TPU v7x, 256 devices: a whole 4x4x8 slice. The times are simulated.
256 devices in a mesh: expert: 32 (over x, y, core), group: 8 (over z).
Axes of the slice: x: 4, y: 4, z: 8, core: 2. Of those that a mesh axis runs over, the one named last changes fastest.
Arguments:
- tokens: bfloat16 [2048, 7168], P(('expert', 'group')), may hold values from -6 to 6
- routes: int32 [2048, 8], P(('expert', 'group')), may hold values from 0 to 31, all different within a row; in each aligned block of 8 rows (0 to 7, 8 to 15, ...) at most 4 rows name the same one
- gate_weight: bfloat16 [32, 7168, 2048], P('expert', None, 'group'), may hold values from -0.0625 to 0.0625
- up_weight: bfloat16 [32, 7168, 2048], P('expert', None, 'group'), may hold values from -0.0625 to 0.0625
- down_weight: bfloat16 [32, 2048, 7168], P('expert', 'group'), may hold values from -6 to 6
- merge_group: int32 [32], replicated, may hold values from 0 to 7, as said below
- neuron_perm: int32 [32, 2048], P('expert', 'group'), may hold values from 0 to 2047, as said below
Outputs:
- merged_down: bfloat16 [8, 2048, 7168], P(None, 'group', 'expert')
Inputs may be any that keep to these rules, and one draw needn't show every extreme that they name: `routes`: among the rows of one device (8 rows), no expert is named by more than 4 rows. `merge_group`: every one of the 8 merge groups has at least one expert. `neuron_perm`: each row is a permutation of 0 to 2047 that keeps every hidden unit within its aligned block of 128.
All inputs are finite; a program needn't handle non-finite values.
Results may differ from a plain program's by a relative error of at most 0.0047.
Values may be sent and summed in bfloat16 or wider, within the bound.
A program may use at most 128 MiB of HBM per device.

v0:
```python
from functools import partial
import jax
import jax.numpy as jnp
from jax import lax
from jax.sharding import PartitionSpec as P

TOP = 8
NB = 128
off_weight = 0.75
ridge_eps = 1e-05


def make_slots(block_routes, block_tokens, experts, capacity):
    row_count = block_tokens.shape[0]
    flat_routes = block_routes.reshape(-1)
    onehot = (flat_routes[:, None] == jnp.arange(experts, dtype=jnp.int32)[None, :]).astype(
        jnp.int32
    )
    position = jnp.sum((jnp.cumsum(onehot, axis=0) - 1) * onehot, axis=1)
    target = flat_routes * capacity + position
    matches = target[None, :] == jnp.arange(experts * capacity, dtype=jnp.int32)[:, None]
    chooser = jnp.sum(
        matches.reshape(experts * capacity, row_count, -1).astype(jnp.float32), axis=2
    ).astype(jnp.bfloat16)
    return jnp.dot(chooser, block_tokens, preferred_element_type=jnp.float32).astype(jnp.bfloat16)


def activate(shard_piece, gate_weight, up_weight):
    gate_part = jnp.einsum(
        "ksjcd,jdf->ksjcf", shard_piece, gate_weight, preferred_element_type=jnp.float32
    )
    up_part = jnp.einsum(
        "ksjcd,jdf->ksjcf", shard_piece, up_weight, preferred_element_type=jnp.float32
    )
    return (jax.nn.silu(gate_part) * up_part).astype(jnp.bfloat16)


def build_system(summed):
    unit_matrix = jnp.eye(summed.shape[-1], dtype=jnp.float32)
    return (
        off_weight * summed + (1.0 - off_weight) * (summed * unit_matrix) + ridge_eps * unit_matrix
    )


def make_inverse(factor):
    unit_matrix = jnp.broadcast_to(jnp.eye(factor.shape[-1], dtype=jnp.float32), factor.shape)
    lower_inverse = lax.linalg.triangular_solve(factor, unit_matrix, left_side=True, lower=True)
    return jnp.einsum(
        "mbki,mbkj->mbij", lower_inverse, lower_inverse, precision=lax.Precision.HIGHEST
    )


def apply_inverse(inverse, right_side):
    return jnp.einsum("mbik,mbkd->mbid", inverse, right_side, precision=lax.Precision.HIGHEST)


def per_device(tokens, routes, gate_weight, up_weight, down_weight, merge_group, neuron_perm):
    expert_count = lax.axis_size("expert")
    group_count = lax.axis_size("group")
    local_experts = gate_weight.shape[0]
    experts = expert_count * local_experts
    row_count = tokens.shape[0]
    width = tokens.shape[1]
    unit_count = gate_weight.shape[2]
    capacity = max(2, row_count * TOP * 2 // (experts * local_experts))
    block_count = unit_count // NB
    column_count = width // expert_count
    groups = experts // 4
    slot_maker = partial(make_slots, experts=experts, capacity=capacity)
    own_slots = slot_maker(routes, tokens).reshape(expert_count, local_experts * capacity, width)
    arrived = lax.all_to_all(own_slots, "expert", split_axis=0, concat_axis=0, tiled=True)
    hidden = activate(
        lax.all_gather(
            arrived.reshape(1, expert_count, local_experts, capacity, width),
            "group",
            axis=0,
            tiled=True,
        ),
        gate_weight,
        up_weight,
    )
    hidden = hidden.reshape(group_count, expert_count, local_experts, capacity, block_count, NB)
    within = (
        neuron_perm.reshape(local_experts, block_count, NB) - lax.axis_index("group") * unit_count
    )
    within = within - (jnp.arange(block_count, dtype=jnp.int32) * NB)[None, :, None]
    selector = (
        within[:, :, None, :] == jnp.arange(NB, dtype=jnp.int32)[None, None, :, None]
    ).astype(jnp.bfloat16)
    aligned = jnp.einsum(
        "gejcbi,jbin->gejcbn", hidden, selector, preferred_element_type=jnp.float32
    ).astype(jnp.bfloat16)
    gram = jnp.einsum("gejcbi,gejcbk->jbik", aligned, aligned, preferred_element_type=jnp.float32)
    moved_rows = jnp.einsum(
        "jbin,jbid->jbnd",
        selector,
        down_weight.reshape(local_experts, block_count, NB, width),
        preferred_element_type=jnp.float32,
    )
    term_part = jnp.einsum("jbni,jbid->jbnd", gram, moved_rows, precision=lax.Precision.HIGHEST)
    owner_index = lax.axis_index("expert")
    own_groups = lax.dynamic_slice_in_dim(merge_group, owner_index * local_experts, local_experts)
    own_onehot = (own_groups[:, None] == jnp.arange(groups, dtype=jnp.int32)[None, :]).astype(
        jnp.float32
    )
    placed = jnp.einsum("jm,jbik->mbik", own_onehot, gram, precision=lax.Precision.HIGHEST)
    group_gram = lax.psum(placed, "expert")
    inverse = make_inverse(jnp.linalg.cholesky(build_system(group_gram)))
    shaped_terms = term_part.reshape(local_experts, block_count, NB, expert_count, column_count)
    collected = lax.all_to_all(shaped_terms, "expert", split_axis=3, concat_axis=0, tiled=True)
    all_onehot = (merge_group[:, None] == jnp.arange(groups, dtype=jnp.int32)[None, :]).astype(
        jnp.float32
    )
    summed = jnp.einsum(
        "em,ebnd->mbnd", all_onehot, collected[:, :, :, 0, :], precision=lax.Precision.HIGHEST
    )
    merged = apply_inverse(inverse, summed)
    return merged.reshape(groups, unit_count, column_count).astype(jnp.bfloat16)


def solution(mesh):
    in_specs = (
        P(("expert", "group"), None),
        P(("expert", "group"), None),
        P("expert", None, "group"),
        P("expert", None, "group"),
        P("expert", "group", None),
        P(),
        P("expert", "group"),
    )
    out_specs = P(None, "group", "expert")
    return jax.shard_map(
        per_device, mesh=mesh, in_specs=in_specs, out_specs=out_specs, check_vma=False
    )
```

profile of v0, /device:TPU:1, one launch (start us, length us, event | category | flops | bytes accessed | tf_op | source)
XLA Modules:
  0.0 783.2 jit_solution(4557623676575485270)
XLA Ops:
  6.5 0.0 copy-start
  6.5 0.0 all-gather.3.cloned.1.call-start
  6.5 0.8 eq.91
  7.3 0.1 fusion.51
  7.4 0.1 reduce_window_sum.11
  7.5 0.2 select_reduce_fusion.1
  7.7 0.1 reduce_sum.21
  7.8 0.7 multiply_add_fusion
  8.5 0.1 convert_reduce_fusion
  8.6 0.0 copy-done
  8.6 0.7 convolution_convert_fusion
  9.3 1.7 reshape.138
  10.9 34.1 %all_to_all.20 = bf16[32,4,7168]{2,1,0:T(4,128)(2,1)S(1)} all-to-all(bf16[32,4,7168]{2,1,0:T(4,128)(2,1)} %reshape.138), channel_id=1, replica_groups=mesh['expert'=32,'group'=8] {'expert'}, dimensions={0} | all-to-all | bytes 3670016 | tf_op jit(solution)/shard_map/all_to_all | solution.py:71
  45.0 0.0 copy-start.3
  45.0 1.8 copy.66
  46.8 0.0 all-gather.3.cloned.1.call-update
  46.8 0.0 copy-done.3
  46.9 0.1 broadcast_subtract_fusion
  46.9 6.1 fusion.44
  53.1 145.8 %all-gather.3.cloned.1.call-done = bf16[256,4,7168]{2,0,1:T(8,128)(2,1)} async-done(((bf16[32,4,7168]{2,0,1:T(8,128)(2,1)}), bf16[256,4,7168]{2,0,1:T(8,128)(2,1)}) %all-gather.3.cloned.1.call-update) | async-done | bytes 14680080 | tf_op jit(solution)/shard_map/all_gather | solution.py:73
  198.9 0.0 copy-start.5
  198.9 8.5 %fusion.14 = f32[8,32,1,4,256]{4,1,3,0,2:T(8,128)S(1)} fusion(bf16[1,7168,256]{2,1,0:T(8,128)(2,1)} %param.9, bf16[8,32,4,7168]{3,1,0,2:T(8,128)(2,1)} %bitcast.99), kind=kOutput, calls=%fused_computation.13 | convolution fusion | flops 3758096384 | bytes 19398656 | tf_op jit(solution)/shard_map/ksjcd,jdf->ksjcf/dot_general | solution.py:29
  207.4 1.9 copy-done.5
  209.3 6.0 fusion.32
  215.3 0.1 reshape.143
  215.5 0.4 fusion.37
  215.8 0.3 convolution_bitcast_fusion
  216.2 14.0 %fusion.57 = f32[2,128,7168]{1,2,0:T(8,128)S(1)} fusion(f32[2,128,128]{2,1,0:T(8,128)S(1)} %convolution_bitcast_fusion, f32[2,128,7168]{2,1,0:T(8,128)} %fusion.44), kind=kOutput, calls=%fused_computation.58 | convolution fusion | flops 2818572288 | bytes 14811136 | tf_op jit(solution)/shard_map/jbni,jbid->jbnd/dot_general | solution.py:100
  230.2 3.7 copy.83
  233.9 0.0 copy-start.4
  233.9 7.9 %all-to-all-start.1 = ((f32[1,2,128,32,224]{2,4,1,0,3:T(8,128)}), f32[1,2,128,32,224]{2,4,1,0,3:T(8,128)}, u32[]{:S(2)}, u32[]{:S(2)}) async-start(f32[1,2,128,32,224]{2,4,1,0,3:T(8,128)} %copy.83), calls=%async_computation.1 | async-start | bytes 14680064 | tf_op jit(solution)/shard_map/all_to_all | solution.py:110
  241.8 0.0 all-reduce.2.cloned.1.call-start
  241.8 0.0 copy-done.4
  241.8 0.6 dynamic_slice.3
  242.4 0.6 compare_convert_fusion
  243.1 0.1 copy.73
  243.2 1.2 broadcast_multiply_fusion
  244.3 0.0 all-reduce.2.cloned.1.call-update
  244.4 0.1 copy.74
  244.5 0.1 copy.75
  244.6 167.6 %all-reduce.2.cloned.1.call-done = f32[8,2,128,128]{2,3,1,0:T(8,128)} async-done(((f32[8,2,128,128]{2,3,1,0:T(8,128)}), f32[8,2,128,128]{2,3,1,0:T(8,128)}) %all-reduce.2.cloned.1.call-update) | async-done | bytes 1048592 | tf_op jit(solution)/shard_map/psum | solution.py:107
  412.2 0.0 copy-start.2
  412.2 1.5 add_add_fusion
  413.7 0.3 copy.76
  414.1 0.0 copy-done.2
  414.1 0.2 fusion.40
  414.3 187.8 %custom-call.7 = f32[8,2,128,128]{3,2,1,0:T(8,128)S(1)} custom-call(f32[8,2,128,128]{3,2,1,0:T(8,128)S(1)} %fusion.40), custom_call_target="Cholesky" | custom-call | tf_op jit(solution)/shard_map/jit(cholesky)/cholesky | solution.py:108
  602.1 0.1 select_reduce_fusion
  602.2 0.2 compare_reduce_fusion
  602.4 0.2 select_bitcast_fusion
  602.6 157.2 %custom-call.8 = f32[8,2,1,128,128]{3,4,2,1,0:T(8,128)S(1)} custom-call(f32[8,2,1,128,128]{4,3,2,1,0:T(8,128)S(1)} %select_bitcast_fusion), custom_call_target="InvertDiagBlocksLowerTriangular" | custom-call | tf_op jit(solution)/shard_map/triangular_solve | solution.py:47
  759.8 1.8 fusion.38
  761.7 1.8 fusion.56
  763.5 0.0 all-to-all-done.1
  763.5 0.0 copy-start.1
  763.5 9.7 %fusion.4 = f32[8,2,128,224]{2,0,3,1:T(8,128)S(1)} fusion(f32[1,2,128,32,224]{2,4,1,0,3:T(8,128)} %all-to-all-done.1, s32[32]{0:T(128)S(1)} %copy-done.4), kind=kOutput, calls=%fused_computation.5 | convolution fusion | flops 176161024 | bytes 9175168 | tf_op jit(solution)/shard_map/em,ebnd->mbnd/dot_general | solution.py:114
  773.3 2.0 fusion.29
  775.3 1.1 copy.127
  776.4 0.0 copy-done.1
  (6 shorter events, 0.1 us)
Async XLA Ops:
  6.5 2.0 copy-start
  6.5 192.3 %all-gather.3.cloned.1.call-start = ((), (), s32[]{:S(2)}) async-start(), calls=%async_computation.3 | async-start | bytes 16515072 | tf_op jit(solution)/shard_map/all_gather | solution.py:73
  45.0 1.9 copy-start.3
  198.9 10.4 %copy-start.5 = (bf16[256,4,7168]{2,0,1:T(8,128)(2,1)S(1)}, bf16[256,4,7168]{2,0,1:T(8,128)(2,1)}, u32[]{:S(2)}) copy-start(bf16[256,4,7168]{2,0,1:T(8,128)(2,1)} %all-gather.3.cloned.1.call-done) | copy-start | bytes 44040196
  233.9 7.9 %copy-start.4 = (s32[32]{0:T(128)S(1)}, s32[32]{0:T(128)}, u32[]{:S(2)}) copy-start(s32[32]{0:T(128)} %param.12) | copy-start | bytes 388
  233.9 529.7 %all-to-all-start.1 = ((f32[1,2,128,32,224]{2,4,1,0,3:T(8,128)}), f32[1,2,128,32,224]{2,4,1,0,3:T(8,128)}, u32[]{:S(2)}, u32[]{:S(2)}) async-start(f32[1,2,128,32,224]{2,4,1,0,3:T(8,128)} %copy.83), calls=%async_computation.1 | async-start | bytes 14680064 | tf_op jit(solution)/shard_map/all_to_all | solution.py:110
  241.8 170.5 %all-reduce.2.cloned.1.call-start = ((), (), s32[]{:S(2)}) async-start(), calls=%async_computation.2 | async-start | bytes 2097152 | tf_op jit(solution)/shard_map/psum | solution.py:107
  412.2 1.8 copy-start.2
  763.5 12.9 %copy-start.1 = (bf16[8,7168]{1,0:T(8,128)(2,1)S(1)}, bf16[8,7168]{1,0:T(8,128)(2,1)}, u32[]{:S(2)}) copy-start(bf16[8,7168]{1,0:T(8,128)(2,1)} %param.7) | copy-start | bytes 344068
Sparse Core Ops, SparseCore 0:
  46.9 151.8 all-gather.2
  245.8 166.4 all-reduce.1
where the time goes:
time: 784 us; the launch traced here: 783 us
  other arithmetic  350 us (45%)
  waiting for transfers between devices  313 us (40%)
  matrix products  51.5 us (7%)
  blocking collectives  34.1 us (4%)
  between operations  13.7 us (2%)
  local copies, waits for them, and re-layouts  12.4 us (2%)
  starting transfers between devices  7.92 us (1%)
    another operation x4, other arithmetic, per_device(): inverse = make_inverse(jnp.linalg.cholesky(build_system(group_gram)))  188 us
    psum x1, waiting for transfers between devices, per_device(): group_gram = lax.psum(placed, 'expert')  168 us
    another operation x3, other arithmetic, make_inverse(): lax.linalg.triangular_solve(factor, unit_matrix, left_side=True, lower=True)  157 us
    all_gather x1, waiting for transfers between devices, per_device(): lax.all_gather(arrived.reshape(1, expert_count, local_experts, capacity,...  146 us
    all_to_all x1, blocking collectives, per_device(): lax.all_to_all(own_slots, 'expert', split_axis=0, concat_axis=0, tiled=True)  34.1 us
  transfers between devices with their start and end apart: 3, of which 2 were waited for; matrix products, arithmetic and copies ran while one was open for 46% of the time, Pallas kernels for 0%

commit v1 on v0

--- a/solution.py
+++ b/solution.py
@@ -70,11 +70,18 @@
     own_slots = slot_maker(routes, tokens).reshape(expert_count, local_experts * capacity, width)
     arrived = lax.all_to_all(own_slots, "expert", split_axis=0, concat_axis=0, tiled=True)
     hidden = activate(
-        lax.all_gather(
-            arrived.reshape(1, expert_count, local_experts, capacity, width),
-            "group",
-            axis=0,
-            tiled=True,
+        jnp.concatenate(
+            lax.all_to_all(
+                jnp.stack(
+                    lax.axis_size("group")
+                    * [arrived.reshape(1, expert_count, local_experts, capacity, width)],
+                    0,
+                ),
+                axis_name="group",
+                split_axis=0,
+                concat_axis=0,
+            ),
+            0,
         ),
         gate_weight,
         up_weight,

time: 784 us -> 962 us (1.23)
  waiting for transfers between devices: 313 us -> 482 us
    all_to_all x0 -> x1, waiting for transfers between devices: none -> 316 us  [per_device(): lax.all_to_all(jnp.stack(lax.axis_size('group') * [arrived.reshape(1, exp...]
    all_gather x1 -> x0, waiting for transfers between devices: 146 us -> none  [per_device(): lax.all_gather(arrived.reshape(1, expert_count, local_experts, capacity,...]
  transfers between devices with their start and end apart: 3 -> 3, of which waited for: 2 -> 2; matrix products, arithmetic and copies ran while one was open for 46% -> 37% of each run, Pallas kernels for 0% -> 0%
where the time goes in v1:
time: 962 us; the launch traced here: 961 us
  waiting for transfers between devices  482 us (50%)
  other arithmetic  350 us (36%)
  matrix products  52.8 us (5%)
  blocking collectives  34.1 us (4%)
  local copies, waits for them, and re-layouts  14.7 us (2%)
  starting transfers between devices  13.7 us (1%)
  between operations  13.7 us (1%)
    all_to_all x1, waiting for transfers between devices, per_device(): lax.all_to_all(jnp.stack(lax.axis_size('group') * [arrived.reshape(1, exp...  316 us
    another operation x4, other arithmetic, per_device(): inverse = make_inverse(jnp.linalg.cholesky(build_system(group_gram)))  188 us
    psum x1, waiting for transfers between devices, per_device(): group_gram = lax.psum(placed, 'expert')  166 us
    another operation x3, other arithmetic, make_inverse(): lax.linalg.triangular_solve(factor, unit_matrix, left_side=True, lower=True)  157 us
    all_to_all x1, blocking collectives, per_device(): lax.all_to_all(own_slots, 'expert', split_axis=0, concat_axis=0, tiled=True)  34.1 us
  transfers between devices with their start and end apart: 3, of which 2 were waited for; matrix products, arithmetic and copies ran while one was open for 37% of the time, Pallas kernels for 0%

profile of v1, /device:TPU:1, one launch (start us, length us, event | category | flops | bytes accessed | tf_op | source)
XLA Modules:
  0.0 961.2 jit_solution(10924694266690464195)
XLA Ops:
  6.5 0.0 copy-start
  6.5 0.8 eq.91
  7.3 0.1 fusion.51
  7.4 0.1 reduce_window_sum.11
  7.5 0.2 select_reduce_fusion.1
  7.7 0.1 reduce_sum.21
  7.8 0.7 multiply_add_fusion
  8.5 0.1 convert_reduce_fusion
  8.6 0.0 copy-done
  8.6 0.7 convolution_convert_fusion
  9.3 1.7 reshape.140
  10.9 34.1 %all_to_all.25 = bf16[32,4,7168]{2,1,0:T(4,128)(2,1)S(1)} all-to-all(bf16[32,4,7168]{2,1,0:T(4,128)(2,1)} %reshape.140), channel_id=1, replica_groups=mesh['expert'=32,'group'=8] {'expert'}, dimensions={0} | all-to-all | bytes 3670016 | tf_op jit(solution)/shard_map/all_to_all | solution.py:71
  45.0 0.5 copy.61
  45.5 5.5 stack.3
  51.0 0.0 copy-start.3
  51.0 8.3 all-to-all-start.1
  59.3 0.0 copy-done.3
  59.4 0.1 broadcast_subtract_fusion
  59.4 6.2 fusion.44
  65.6 316.2 %all-to-all-done.1 = bf16[8,1,32,1,4,7168]{5,2,4,3,1,0:T(8,128)(2,1)} async-done(((bf16[8,1,32,1,4,7168]{5,2,4,3,1,0:T(8,128)(2,1)}), bf16[8,1,32,1,4,7168]{5,2,4,3,1,0:T(8,128)(2,1)}, u32[]{:S(2)}, u32[]{:S(2)}) %all-to-all-start.1) | async-done | bytes 14680096 | tf_op jit(solution)/shard_map/all_to_all | solution.py:74
  381.8 0.0 copy-start.5
  381.8 8.5 fusion.14
  390.3 0.0 copy-done.5
  390.3 7.5 fusion.32
  397.8 0.1 reshape.144
  398.0 0.4 fusion.37
  398.3 0.3 convolution_bitcast_fusion
  398.7 13.8 %fusion.57 = f32[2,128,7168]{1,2,0:T(8,128)S(1)} fusion(f32[2,128,128]{2,1,0:T(8,128)S(1)} %convolution_bitcast_fusion, f32[2,128,7168]{2,1,0:T(8,128)} %fusion.44), kind=kOutput, calls=%fused_computation.58 | convolution fusion | flops 2818572288 | bytes 14811136 | tf_op jit(solution)/shard_map/jbni,jbid->jbnd/dot_general | solution.py:107
  412.5 3.7 copy.76
  416.2 0.0 copy-start.4
  416.2 5.3 all-to-all-start.2
  421.5 0.0 all-reduce.2.cloned.1.call-start
  421.6 0.0 copy-done.4
  421.6 0.6 dynamic_slice.3
  422.2 0.6 compare_convert_fusion
  422.8 0.1 copy.66
  422.9 1.2 broadcast_multiply_fusion
  424.1 0.0 all-reduce.2.cloned.1.call-update
  424.1 0.1 copy.67
  424.2 0.1 copy.68
  424.4 166.0 %all-reduce.2.cloned.1.call-done = f32[8,2,128,128]{2,3,1,0:T(8,128)} async-done(((f32[8,2,128,128]{2,3,1,0:T(8,128)}), f32[8,2,128,128]{2,3,1,0:T(8,128)}) %all-reduce.2.cloned.1.call-update) | async-done | bytes 1048592 | tf_op jit(solution)/shard_map/psum | solution.py:114
  590.4 0.0 copy-start.2
  590.4 1.5 add_add_fusion
  591.9 0.3 copy.69
  592.2 0.0 copy-done.2
  592.2 0.2 fusion.40
  592.5 187.6 %custom-call.7 = f32[8,2,128,128]{3,2,1,0:T(8,128)S(1)} custom-call(f32[8,2,128,128]{3,2,1,0:T(8,128)S(1)} %fusion.40), custom_call_target="Cholesky" | custom-call | tf_op jit(solution)/shard_map/jit(cholesky)/cholesky | solution.py:115
  780.0 0.1 select_reduce_fusion
  780.1 0.2 compare_reduce_fusion
  780.3 0.2 select_bitcast_fusion
  780.6 157.2 %custom-call.8 = f32[8,2,1,128,128]{3,4,2,1,0:T(8,128)S(1)} custom-call(f32[8,2,1,128,128]{4,3,2,1,0:T(8,128)S(1)} %select_bitcast_fusion), custom_call_target="InvertDiagBlocksLowerTriangular" | custom-call | tf_op jit(solution)/shard_map/triangular_solve | solution.py:47
  937.8 1.8 fusion.38
  939.6 1.8 fusion.56
  941.4 0.0 all-to-all-done.2
  941.5 0.0 copy-start.1
  941.5 9.7 %fusion.4 = f32[8,2,128,224]{2,0,3,1:T(8,128)S(1)} fusion(f32[1,2,128,32,224]{2,4,1,0,3:T(8,128)} %all-to-all-done.2, s32[32]{0:T(128)S(1)} %copy-done.4), kind=kOutput, calls=%fused_computation.5 | convolution fusion | flops 176161024 | bytes 9175168 | tf_op jit(solution)/shard_map/em,ebnd->mbnd/dot_general | solution.py:121
  951.2 2.0 fusion.29
  953.2 1.1 copy.108
  954.3 0.0 copy-done.1
  (6 shorter events, 0.1 us)
Async XLA Ops:
  6.5 2.0 copy-start
  51.0 8.3 copy-start.3
  51.0 330.7 %all-to-all-start.1 = ((bf16[8,1,32,1,4,7168]{5,2,4,3,1,0:T(8,128)(2,1)}), bf16[8,1,32,1,4,7168]{5,2,4,3,1,0:T(8,128)(2,1)}, u32[]{:S(2)}, u32[]{:S(2)}) async-start(bf16[8,1,32,1,4,7168]{5,2,4,3,1,0:T(8,128)(2,1)} %stack.3), calls=%async_computation.1 | async-start | bytes 29360128 | tf_op jit(solution)/shard_map/all_to_all | solution.py:74
  381.8 8.5 copy-start.5
  416.2 5.4 copy-start.4
  416.2 525.2 %all-to-all-start.2 = ((f32[1,2,128,32,224]{2,4,1,0,3:T(8,128)}), f32[1,2,128,32,224]{2,4,1,0,3:T(8,128)}, u32[]{:S(2)}, u32[]{:S(2)}) async-start(f32[1,2,128,32,224]{2,4,1,0,3:T(8,128)} %copy.76), calls=%async_computation.2 | async-start | bytes 14680064 | tf_op jit(solution)/shard_map/all_to_all | solution.py:117
  421.5 168.9 %all-reduce.2.cloned.1.call-start = ((), (), s32[]{:S(2)}) async-start(), calls=%async_computation.3 | async-start | bytes 2097152 | tf_op jit(solution)/shard_map/psum | solution.py:114
  590.4 1.8 copy-start.2
  941.5 12.9 %copy-start.1 = (bf16[8,7168]{1,0:T(8,128)(2,1)S(1)}, bf16[8,7168]{1,0:T(8,128)(2,1)}, u32[]{:S(2)}) copy-start(bf16[8,7168]{1,0:T(8,128)(2,1)} %param.7) | copy-start | bytes 344068
Sparse Core Ops, SparseCore 0:
  425.6 164.7 all-reduce.1
